TPU v7x, 32 devices: a whole 2x2x4 slice. The times are simulated.
32 devices in a mesh: cols: 4 (over y, x), rows: 8 (over z, core).
Axes of the slice: x: 2, y: 2, z: 4, core: 2. Of those that a mesh axis runs over, the one named last changes fastest.
Arguments:
- gradient: float32 [128, 8192], P('cols', 'rows'), may hold values from -100 to 100
- width_factor: float32 [128, 128], P(None, 'cols'), may hold values from -3 to 4, as said below
- diag_blocks: float32 [64, 128, 128], P('rows'), may hold values from -2 to 24, as said below
- jacobi_inverse: float32 [64, 128, 128], P('rows'), may hold values from -2 to 2, as said below
- coupling_tiles: bfloat16 [32, 128, 128], P('rows'), may hold values from -4 to 4, as said below
- tile_local: int32 [32], P('rows'), may hold values from 0 to 7
- tile_remote: int32 [32], P('rows'), may hold values from 0 to 63, as said below
- tile_count: int32 [8], P('rows'), may hold values from 0 to 3, as said below
Outputs:
- solution: float32 [128, 8192], P('cols', 'rows')
- residual: float32 [128, 8192], P('cols', 'rows')
Inputs may be any that keep to these rules, and one draw needn't show every extreme that they name: `tile_remote`: the live entries are the first tile_count entries of each device's list; they name distinct devices other than the owner, each at most once. For a live entry of device d naming block J of device e, device e has a live entry naming d's block with its tile the transpose. Pad entries hold valid indices. `tile_count`: at most 3 on one device, reached on some device. `coupling_tiles`: with diag_blocks and the live entries, M is symmetric positive definite. `diag_blocks`: symmetric positive definite tiles. `jacobi_inverse`: the inverses of diag_blocks, symmetric. `width_factor`: symmetric positive definite.
All inputs are finite; a program needn't handle non-finite values.
Results may differ from a plain program's by a relative error of at most 0.0085.
Values may be sent and summed in bfloat16 or wider, within the bound.
No kernel may reach another device: no remote copies, remote signals or barrier semaphores. Data moves between devices by JAX's collectives and lax.ppermute only.
A program may use at most 64 MiB of HBM per device.

v0:
```python
import jax
import jax.numpy as jnp
from jax import lax
from jax.sharding import PartitionSpec as P

BLOCK = 128
ITERS = 6
highest = lax.Precision.HIGHEST


def on_device(
    gradient,
    width_factor,
    diag_blocks,
    jacobi_inverse,
    coupling_tiles,
    tile_local,
    tile_remote,
    tile_count,
):
    width_dev, rows_dev = gradient.shape
    blocks_dev = diag_blocks.shape[0]
    slot_count = tile_local.shape[0]
    devices = lax.axis_size("rows")
    active_slot = jnp.arange(slot_count, dtype=jnp.int32) < tile_count[0]
    placing = (
        (tile_local[:, None] == jnp.arange(blocks_dev, dtype=jnp.int32)[None, :])
        & active_slot[:, None]
    ).astype(jnp.float32)
    owner_dev = tile_remote // blocks_dev
    matches = active_slot[:, None] & (
        owner_dev[:, None] == jnp.arange(devices, dtype=jnp.int32)[None, :]
    )
    request = jnp.sum(jnp.where(matches, (tile_remote % blocks_dev)[:, None], 0), axis=0)
    granted = lax.all_to_all(request, "rows", split_axis=0, concat_axis=0, tiled=True)

    def precondition(vector):
        blocks = vector.reshape(width_dev, blocks_dev, BLOCK)
        return jnp.einsum("enj,nji->eni", blocks, jacobi_inverse, precision=highest).reshape(
            width_dev, rows_dev
        )

    solution = jnp.zeros_like(gradient)
    residual = gradient
    precond_res = precondition(residual)
    direction = precond_res
    res_norm = lax.psum(jnp.sum(residual * precond_res), ("cols", "rows"))
    for iteration in range(ITERS):
        apply_blocks = direction.reshape(width_dev, blocks_dev, BLOCK)
        local_part = jnp.einsum("enj,nji->eni", apply_blocks, diag_blocks, precision=highest)
        rounded = direction.astype(jnp.bfloat16).reshape(width_dev, blocks_dev, BLOCK)
        incoming = lax.all_to_all(
            rounded[:, granted, :], "rows", split_axis=1, concat_axis=1, tiled=True
        )
        sources = incoming[:, owner_dev, :]
        products = jnp.einsum(
            "ekj,kji->eki", sources, coupling_tiles, preferred_element_type=jnp.float32
        )
        coupled = jnp.einsum("eki,kb->ebi", products, placing, precision=highest)
        summed = lax.psum(
            jnp.dot(
                width_factor, (local_part + coupled).reshape(width_dev, rows_dev), precision=highest
            ),
            "cols",
        )
        fisher_dir = lax.dynamic_slice_in_dim(
            summed, lax.axis_index("cols") * width_dev, width_dev, 0
        )
        precond_fisher = precondition(fisher_dir)
        curvature, cross_term, second_term = lax.psum(
            (
                jnp.sum(direction * fisher_dir),
                jnp.sum(fisher_dir * precond_res),
                jnp.sum(fisher_dir * precond_fisher),
            ),
            ("cols", "rows"),
        )
        step_size = res_norm / curvature
        solution = solution + step_size * direction
        residual = residual - step_size * fisher_dir
        if iteration + 1 < ITERS:
            precond_res = precond_res - step_size * precond_fisher
            next_norm = (
                res_norm - 2.0 * step_size * cross_term + step_size * step_size * second_term
            )
            direction = precond_res + next_norm / res_norm * direction
            res_norm = next_norm
    return (solution, residual)


def solution(mesh):
    placed = (
        P("cols", "rows"),
        P(None, "cols"),
        P("rows", None, None),
        P("rows", None, None),
        P("rows", None, None),
        P("rows"),
        P("rows"),
        P("rows"),
    )
    return jax.shard_map(
        on_device,
        mesh=mesh,
        in_specs=placed,
        out_specs=(P("cols", "rows"), P("cols", "rows")),
        check_vma=False,
    )
```

profile of v0, /device:TPU:0, one launch (start us, length us, event | category | flops | bytes accessed | tf_op | source)
XLA Modules:
  0.0 644.4 jit_solution(5383939424549361704)
XLA Ops:
  7.9 0.6 copy-done.6
  8.6 0.7 copy.175
  9.3 6.4 all-to-all-start
  15.7 1.5 bitcast_convert_fusion
  17.2 4.0 all-to-all-done
  21.4 1.2 gather_fusion
  22.6 3.4 all-to-all-start.1
  26.1 5.7 all-to-all-done.1
  31.8 0.6 gather_fusion.1
  32.6 0.3 fusion.73
  32.8 0.6 fusion.5
  33.6 1.4 convolution_bitcast_fusion.5
  35.1 44.0 %all-reduce.12.cloned.1.call-done = f32[128,1024]{1,0:T(8,128)} async-done(((f32[128,1024]{1,0:T(8,128)}), f32[128,1024]{1,0:T(8,128)}) %all-reduce.12.cloned.1.call-update) | async-done | bytes 524304 | tf_op jit(solution)/shard_map/psum | solution.py:60
  79.0 1.5 fusion.49
  80.5 1.6 fusion.25
  82.1 39.6 %all-reduce.4 = (f32[]{:T(128)}, f32[]{:T(128)}, f32[]{:T(128)}) all-reduce(f32[]{:T(128)} %get-tuple-element.24, f32[]{:T(128)} %get-tuple-element.23, f32[]{:T(128)} %get-tuple-element.22), channel_id=1, replica_groups=mesh['cols'=4,'rows'=8] {'cols','rows'}, use_global_device_ids=true, to_apply=%region_1.2 | all-reduce | flops 3 | bytes 24 | tf_op jit(solution)/shard_map/psum | solution.py:47
  125.5 0.6 gather_fusion.2
  126.0 9.3 %all_to_all.42 = bf16[32,8,128]{2,0,1:T(8,128)(2,1)S(1)} all-to-all(bf16[32,8,128]{2,0,1:T(8,128)(2,1)S(1)} %bitcast.343), channel_id=1, replica_groups=mesh['cols'=4,'rows'=8] {'rows'}, dimensions={1} | all-to-all | bytes 131072 | tf_op jit(solution)/shard_map/all_to_all | solution.py:52
  135.3 0.6 gather_fusion.3
  136.3 0.6 fusion.4
  136.9 1.4 convolution_bitcast_fusion.4
  138.4 45.0 %all-reduce.14.cloned.1.call-done = f32[128,1024]{1,0:T(8,128)} async-done(((f32[128,1024]{1,0:T(8,128)}), f32[128,1024]{1,0:T(8,128)}) %all-reduce.14.cloned.1.call-update) | async-done | bytes 524304 | tf_op jit(solution)/shard_map/psum | solution.py:60
  183.4 1.5 fusion.46
  184.9 0.8 fusion.21
  185.7 39.6 %all-reduce.3 = (f32[]{:T(128)}, f32[]{:T(128)}, f32[]{:T(128)}) all-reduce(f32[]{:T(128)} %get-tuple-element.21, f32[]{:T(128)} %get-tuple-element.20, f32[]{:T(128)} %get-tuple-element.19), channel_id=1, replica_groups=mesh['cols'=4,'rows'=8] {'cols','rows'}, use_global_device_ids=true, to_apply=%region_10.11 | all-reduce | flops 3 | bytes 24 | tf_op jit(solution)/shard_map/psum | solution.py:70
  227.3 0.6 gather_fusion.4
  227.8 9.3 %all_to_all.43 = bf16[32,8,128]{2,0,1:T(8,128)(2,1)S(1)} all-to-all(bf16[32,8,128]{2,0,1:T(8,128)(2,1)S(1)} %bitcast.344), channel_id=1, replica_groups=mesh['cols'=4,'rows'=8] {'rows'}, dimensions={1} | all-to-all | bytes 131072 | tf_op jit(solution)/shard_map/all_to_all | solution.py:52
  237.1 0.6 gather_fusion.5
  237.8 0.3 fusion.69
  238.1 0.6 fusion.3
  238.6 1.4 convolution_bitcast_fusion.3
  240.2 45.0 %all-reduce.16.cloned.1.call-done = f32[128,1024]{1,0:T(8,128)} async-done(((f32[128,1024]{1,0:T(8,128)}), f32[128,1024]{1,0:T(8,128)}) %all-reduce.16.cloned.1.call-update) | async-done | bytes 524304 | tf_op jit(solution)/shard_map/psum | solution.py:60
  285.2 1.5 fusion.43
  286.6 1.7 multiply_reduce_fusion.5
  288.3 39.6 %all-reduce.2 = (f32[]{:T(128)}, f32[]{:T(128)}, f32[]{:T(128)}) all-reduce(f32[]{:T(128)} %get-tuple-element.13, f32[]{:T(128)} %get-tuple-element.12, f32[]{:T(128)} %get-tuple-element.18), channel_id=1, replica_groups=mesh['cols'=4,'rows'=8] {'cols','rows'}, use_global_device_ids=true, to_apply=%region_17.18 | all-reduce | flops 3 | bytes 24 | tf_op jit(solution)/shard_map/psum | solution.py:70
  329.9 0.6 gather_fusion.6
  330.4 9.3 %all_to_all.44 = bf16[32,8,128]{2,0,1:T(8,128)(2,1)S(1)} all-to-all(bf16[32,8,128]{2,0,1:T(8,128)(2,1)S(1)} %bitcast.345), channel_id=1, replica_groups=mesh['cols'=4,'rows'=8] {'rows'}, dimensions={1} | all-to-all | bytes 131072 | tf_op jit(solution)/shard_map/all_to_all | solution.py:52
  339.7 0.6 gather_fusion.7
  340.7 0.6 fusion.2
  341.3 1.4 convolution_bitcast_fusion.2
  342.8 45.0 %all-reduce.18.cloned.1.call-done = f32[128,1024]{1,0:T(8,128)} async-done(((f32[128,1024]{1,0:T(8,128)}), f32[128,1024]{1,0:T(8,128)}) %all-reduce.18.cloned.1.call-update) | async-done | bytes 524304 | tf_op jit(solution)/shard_map/psum | solution.py:60
  387.8 1.5 fusion.40
  389.2 1.6 fusion.13
  390.8 39.7 %all-reduce.1 = (f32[]{:T(128)}, f32[]{:T(128)}, f32[]{:T(128)}) all-reduce(f32[]{:T(128)} %get-tuple-element.17, f32[]{:T(128)} %get-tuple-element.16, f32[]{:T(128)} %get-tuple-element.15), channel_id=1, replica_groups=mesh['cols'=4,'rows'=8] {'cols','rows'}, use_global_device_ids=true, to_apply=%region_24.25 | all-reduce | flops 3 | bytes 24 | tf_op jit(solution)/shard_map/psum | solution.py:70
  432.7 0.6 gather_fusion.8
  433.2 9.3 %all_to_all.45 = bf16[32,8,128]{2,0,1:T(8,128)(2,1)S(1)} all-to-all(bf16[32,8,128]{2,0,1:T(8,128)(2,1)S(1)} %bitcast.346), channel_id=1, replica_groups=mesh['cols'=4,'rows'=8] {'rows'}, dimensions={1} | all-to-all | bytes 131072 | tf_op jit(solution)/shard_map/all_to_all | solution.py:52
  442.5 0.6 gather_fusion.9
  443.2 0.3 fusion.65
  443.5 0.6 fusion.1
  444.0 1.4 convolution_bitcast_fusion.1
  445.5 45.1 %all-reduce.20.cloned.1.call-done = f32[128,1024]{1,0:T(8,128)} async-done(((f32[128,1024]{1,0:T(8,128)}), f32[128,1024]{1,0:T(8,128)}) %all-reduce.20.cloned.1.call-update) | async-done | bytes 524304 | tf_op jit(solution)/shard_map/psum | solution.py:60
  490.6 1.5 fusion.37
  492.1 1.6 multiply_reduce_fusion.1
  493.6 39.6 %all-reduce = (f32[]{:T(128)}, f32[]{:T(128)}, f32[]{:T(128)}) all-reduce(f32[]{:T(128)} %get-tuple-element.11, f32[]{:T(128)} %get-tuple-element.10, f32[]{:T(128)} %get-tuple-element.14), channel_id=1, replica_groups=mesh['cols'=4,'rows'=8] {'cols','rows'}, use_global_device_ids=true, to_apply=%region_31.32 | all-reduce | flops 3 | bytes 24 | tf_op jit(solution)/shard_map/psum | solution.py:70
  535.2 0.6 gather_fusion.10
  535.8 9.3 %all_to_all.46 = bf16[32,8,128]{2,0,1:T(8,128)(2,1)S(1)} all-to-all(bf16[32,8,128]{2,0,1:T(8,128)(2,1)S(1)} %bitcast.342), channel_id=1, replica_groups=mesh['cols'=4,'rows'=8] {'rows'}, dimensions={1} | all-to-all | bytes 131072 | tf_op jit(solution)/shard_map/all_to_all | solution.py:52
  545.1 0.6 gather_fusion.11
  546.1 0.6 fusion
  546.6 1.4 convolution_bitcast_fusion
  548.1 45.1 %all-reduce.22.cloned.1.call-done = f32[128,1024]{1,0:T(8,128)} async-done(((f32[128,1024]{1,0:T(8,128)}), f32[128,1024]{1,0:T(8,128)}) %all-reduce.22.cloned.1.call-update) | async-done | bytes 524304 | tf_op jit(solution)/shard_map/psum | solution.py:60
  593.2 1.5 multiply_reduce_fusion
  594.7 39.5 %psum.178 = f32[]{:T(128)} all-reduce(f32[]{:T(128)} %multiply_reduce_fusion), channel_id=1, replica_groups=mesh['cols'=4,'rows'=8] {'cols','rows'}, use_global_device_ids=true, to_apply=%region_38.39 | all-reduce | flops 1 | bytes 8 | tf_op jit(solution)/shard_map/psum | solution.py:70
  634.9 0.7 fusion.35
  635.7 1.9 multiply_subtract_fusion
  (49 shorter events, 2.8 us)
Async XLA Ops:
  7.2 8.5 %copy-start = (f32[8,128,128]{2,1,0:T(8,128)S(1)}, f32[8,128,128]{2,1,0:T(8,128)}, u32[]{:S(2)}) copy-start(f32[8,128,128]{2,1,0:T(8,128)} %param.11) | copy-start | bytes 1572868
  7.9 0.7 copy-start.6
  9.3 11.9 %all-to-all-start = ((s32[8,1,1]{2,1,0:T(1,128)}), s32[8,1,1]{2,1,0:T(1,128)S(1)}, u32[]{:S(2)}, u32[]{:S(2)}) async-start(s32[8,1,1]{2,1,0:T(1,128)} %copy.175), calls=%async_computation | async-start | bytes 8192 | tf_op jit(solution)/shard_map/all_to_all | solution.py:35
  15.7 10.4 %copy-start.7 = (s32[4]{0:T(128)S(1)}, s32[4]{0:T(128)}, u32[]{:S(2)}) copy-start(s32[4]{0:T(128)} %param.13) | copy-start | bytes 52
  15.7 16.7 %copy-start.2 = (bf16[4,128,128]{2,1,0:T(8,128)(2,1)S(1)}, bf16[4,128,128]{2,1,0:T(8,128)(2,1)}, u32[]{:S(2)}) copy-start(bf16[4,128,128]{2,1,0:T(8,128)(2,1)} %param.12) | copy-start | bytes 393220
  17.2 15.6 %copy-start.1 = (f32[8,128,128]{2,1,0:T(8,128)S(1)}, f32[8,128,128]{2,1,0:T(8,128)}, u32[]{:S(2)}) copy-start(f32[8,128,128]{2,1,0:T(8,128)} %param.10) | copy-start | bytes 1572868
  22.6 9.2 %all-to-all-start.1 = ((bf16[32,8,128]{2,0,1:T(8,128)(2,1)}), bf16[32,8,128]{2,0,1:T(8,128)(2,1)S(1)}, u32[]{:S(2)}, u32[]{:S(2)}) async-start(bf16[32,8,128]{2,0,1:T(8,128)(2,1)} %bitcast.5), calls=%async_computation.1 | async-start | bytes 131072 | tf_op jit(solution)/shard_map/all_to_all | solution.py:52
  26.0 53.0 %all-reduce.12.cloned.1.call-start = ((), (), s32[]{:S(2)}) async-start(), calls=%async_computation.7 | async-start | bytes 1048576 | tf_op jit(solution)/shard_map/psum | solution.py:60
  32.8 0.7 copy-start.4
  35.0 148.4 %all-reduce.14.cloned.1.call-start = ((), (), s32[]{:S(2)}) async-start(), calls=%async_computation.8 | async-start | bytes 1048576 | tf_op jit(solution)/shard_map/psum | solution.py:60
  35.1 45.4 %copy-start.3 = (f32[32,1024]{1,0:T(8,128)S(1)}, f32[32,1024]{1,0:T(8,128)}, u32[]{:S(2)}) copy-start(f32[32,1024]{1,0:T(8,128)} %param.8) | copy-start | bytes 393220
  138.3 146.9 %all-reduce.16.cloned.1.call-start = ((), (), s32[]{:S(2)}) async-start(), calls=%async_computation.9 | async-start | bytes 1048576 | tf_op jit(solution)/shard_map/psum | solution.py:60
  183.4 1.5 copy-start.5
  240.1 147.7 %all-reduce.18.cloned.1.call-start = ((), (), s32[]{:S(2)}) async-start(), calls=%async_computation.10 | async-start | bytes 1048576 | tf_op jit(solution)/shard_map/psum | solution.py:60
  342.7 147.9 %all-reduce.20.cloned.1.call-start = ((), (), s32[]{:S(2)}) async-start(), calls=%async_computation.11 | async-start | bytes 1048576 | tf_op jit(solution)/shard_map/psum | solution.py:60
  445.5 147.7 %all-reduce.22.cloned.1.call-start = ((), (), s32[]{:S(2)}) async-start(), calls=%async_computation.12 | async-start | bytes 1048576 | tf_op jit(solution)/shard_map/psum | solution.py:60
Sparse Core Ops, SparseCore 0:
  35.1 43.8 all-reduce.11
  138.4 44.9 all-reduce.13
  240.2 44.9 all-reduce.15
  342.8 44.8 all-reduce.17
  445.6 44.9 all-reduce.19
  548.2 44.9 all-reduce.21
where the time goes:
time: 646 us; the launch traced here: 644 us
  blocking collectives  284 us (44%)
  waiting for transfers between devices  279 us (43%)
  between operations  27.4 us (4%)
  matrix products  23.3 us (4%)
  other arithmetic  12 us (2%)
  starting transfers between devices  9.95 us (2%)
  local copies, waits for them, and re-layouts  8.86 us (1%)
    psum x6, waiting for transfers between devices, on_device(): lax.psum(jnp.dot(width_factor, (local_part + coupled).reshape(width_dev,...  269 us
    psum x5, blocking collectives, on_device(): lax.psum((jnp.sum(direction * fisher_dir), jnp.sum(fisher_dir * precond_r...  198 us
    all_to_all x5, blocking collectives, on_device(): lax.all_to_all(rounded[:, granted, :], 'rows', split_axis=1, concat_axis=...  46.4 us
    psum x1, blocking collectives, on_device(): res_norm = lax.psum(jnp.sum(residual * precond_res), ('cols', 'rows'))  39.6 us
  transfers between devices with their start and end apart: 8, of which 8 were waited for; matrix products, arithmetic and copies ran while one was open for 0% of the time, Pallas kernels for 0%

commit v1 on v0

--- a/solution.py
+++ b/solution.py
@@ -67,13 +67,16 @@
             summed, lax.axis_index("cols") * width_dev, width_dev, 0
         )
         precond_fisher = precondition(fisher_dir)
-        curvature, cross_term, second_term = lax.psum(
-            (
-                jnp.sum(direction * fisher_dir),
-                jnp.sum(fisher_dir * precond_res),
-                jnp.sum(fisher_dir * precond_fisher),
+        curvature, cross_term, second_term = jax.lax.psum(
+            jax.lax.psum(
+                (
+                    jnp.sum(direction * fisher_dir),
+                    jnp.sum(fisher_dir * precond_res),
+                    jnp.sum(fisher_dir * precond_fisher),
+                ),
+                "cols",
             ),
-            ("cols", "rows"),
+            "rows",
         )
         step_size = res_norm / curvature
         solution = solution + step_size * direction

time: 646 us -> 577 us (0.89)
  blocking collectives: 284 us -> 227 us
  waiting for transfers between devices: 279 us -> 268 us
    psum x5 -> x12, blocking collectives: 198 us -> 146 us  [the longest x6 86.4 us: on_device(): jax.lax.psum(jax.lax.psum((jnp.sum(direction * fisher_dir), jnp.sum(fishe...]
    psum x6, waiting for transfers between devices: 269 us -> 258 us  [on_device(): lax.psum(jnp.dot(width_factor, (local_part + coupled).reshape(width_dev,...]
where the time goes in v1:
time: 577 us; the launch traced here: 576 us
  waiting for transfers between devices  268 us (46%)
  blocking collectives  227 us (39%)
  between operations  27.4 us (5%)
  matrix products  23.3 us (4%)
  other arithmetic  11.9 us (2%)
  starting transfers between devices  9.96 us (2%)
  local copies, waits for them, and re-layouts  8.86 us (2%)
    psum x6, waiting for transfers between devices, on_device(): lax.psum(jnp.dot(width_factor, (local_part + coupled).reshape(width_dev,...  258 us
    psum x6, blocking collectives, on_device(): jax.lax.psum(jax.lax.psum((jnp.sum(direction * fisher_dir), jnp.sum(fishe...  86.4 us
    psum x6, blocking collectives, on_device(): jax.lax.psum((jnp.sum(direction * fisher_dir), jnp.sum(fisher_dir * preco...  59.3 us
    all_to_all x5, blocking collectives, on_device(): lax.all_to_all(rounded[:, granted, :], 'rows', split_axis=1, concat_axis=...  41.5 us
    psum x1, blocking collectives, on_device(): res_norm = lax.psum(jnp.sum(residual * precond_res), ('cols', 'rows'))  39.5 us
  transfers between devices with their start and end apart: 8, of which 8 were waited for; matrix products, arithmetic and copies ran while one was open for 0% of the time, Pallas kernels for 0%

profile of v1, /device:TPU:0, one launch (start us, length us, event | category | flops | bytes accessed | tf_op | source)
XLA Modules:
  0.0 576.0 jit_solution(3620687472115969727)
XLA Ops:
  7.9 0.6 copy-done.6
  8.6 0.7 copy.175
  9.3 6.4 %all-to-all-start = ((s32[8,1,1]{2,1,0:T(1,128)}), s32[8,1,1]{2,1,0:T(1,128)S(1)}, u32[]{:S(2)}, u32[]{:S(2)}) async-start(s32[8,1,1]{2,1,0:T(1,128)} %copy.175), calls=%async_computation | async-start | bytes 8192 | tf_op jit(solution)/shard_map/all_to_all | solution.py:35
  15.7 1.5 bitcast_convert_fusion
  17.2 4.0 all-to-all-done
  21.4 1.2 gather_fusion
  22.6 3.4 all-to-all-start.1
  26.1 5.7 all-to-all-done.1
  31.8 0.6 gather_fusion.1
  32.8 0.6 fusion.5
  33.6 1.4 convolution_bitcast_fusion.5
  35.1 44.0 %all-reduce.17.cloned.1.call-done = f32[128,1024]{1,0:T(8,128)} async-done(((f32[128,1024]{1,0:T(8,128)}), f32[128,1024]{1,0:T(8,128)}) %all-reduce.17.cloned.1.call-update) | async-done | bytes 524304 | tf_op jit(solution)/shard_map/psum | solution.py:60
  79.0 1.5 fusion.49
  80.5 1.6 fusion.25
  82.1 39.5 %psum.265 = f32[]{:T(128)} all-reduce(f32[]{:T(128)} %get-tuple-element.24), channel_id=1, replica_groups=mesh['cols'=4,'rows'=8] {'cols','rows'}, use_global_device_ids=true, to_apply=%region_1.2 | all-reduce | flops 1 | bytes 8 | tf_op jit(solution)/shard_map/psum | solution.py:47
  121.6 11.4 %all-reduce.9 = (f32[]{:T(128)}, f32[]{:T(128)}) all-reduce(f32[]{:T(128)} %get-tuple-element.23, f32[]{:T(128)} %get-tuple-element.22), channel_id=1, replica_groups=mesh['cols'=4,'rows'=8] {'cols'}, use_global_device_ids=true, to_apply=%region_5.6 | all-reduce | flops 2 | bytes 16 | tf_op jit(solution)/shard_map/psum | solution.py:71
  133.1 14.2 %all-reduce.4 = (f32[]{:T(128)}, f32[]{:T(128)}) all-reduce(f32[]{:T(128)} %get-tuple-element.51, f32[]{:T(128)} %get-tuple-element.52), channel_id=1, replica_groups=mesh['cols'=4,'rows'=8] {'rows'}, use_global_device_ids=true, to_apply=%region_6.7 | all-reduce | flops 2 | bytes 16 | tf_op jit(solution)/shard_map/psum | solution.py:70
  151.0 0.6 gather_fusion.2
  151.6 8.3 %all_to_all.42 = bf16[32,8,128]{2,0,1:T(8,128)(2,1)S(1)} all-to-all(bf16[32,8,128]{2,0,1:T(8,128)(2,1)S(1)} %bitcast.343), channel_id=1, replica_groups=mesh['cols'=4,'rows'=8] {'rows'}, dimensions={1} | all-to-all | bytes 131072 | tf_op jit(solution)/shard_map/all_to_all | solution.py:52
  159.9 0.6 gather_fusion.3
  160.9 0.6 fusion.4
  161.4 1.4 convolution_bitcast_fusion.4
  163.0 42.1 %all-reduce.19.cloned.1.call-done = f32[128,1024]{1,0:T(8,128)} async-done(((f32[128,1024]{1,0:T(8,128)}), f32[128,1024]{1,0:T(8,128)}) %all-reduce.19.cloned.1.call-update) | async-done | bytes 524304 | tf_op jit(solution)/shard_map/psum | solution.py:60
  205.0 1.5 fusion.46
  206.6 0.7 fusion.21
  207.2 9.6 %all-reduce.8 = (f32[]{:T(128)}, f32[]{:T(128)}, f32[]{:T(128)}) all-reduce(f32[]{:T(128)} %get-tuple-element.21, f32[]{:T(128)} %get-tuple-element.20, f32[]{:T(128)} %get-tuple-element.19), channel_id=1, replica_groups=mesh['cols'=4,'rows'=8] {'cols'}, use_global_device_ids=true, to_apply=%region_12.13 | all-reduce | flops 3 | bytes 24 | tf_op jit(solution)/shard_map/psum | solution.py:71
  216.9 14.4 %all-reduce.3 = (f32[]{:T(128)}, f32[]{:T(128)}, f32[]{:T(128)}) all-reduce(f32[]{:T(128)} %get-tuple-element.48, f32[]{:T(128)} %get-tuple-element.49, f32[]{:T(128)} %get-tuple-element.50), channel_id=1, replica_groups=mesh['cols'=4,'rows'=8] {'rows'}, use_global_device_ids=true, to_apply=%region_13.14 | all-reduce | flops 3 | bytes 24 | tf_op jit(solution)/shard_map/psum | solution.py:70
  233.3 0.6 gather_fusion.4
  233.9 8.3 %all_to_all.43 = bf16[32,8,128]{2,0,1:T(8,128)(2,1)S(1)} all-to-all(bf16[32,8,128]{2,0,1:T(8,128)(2,1)S(1)} %bitcast.344), channel_id=1, replica_groups=mesh['cols'=4,'rows'=8] {'rows'}, dimensions={1} | all-to-all | bytes 131072 | tf_op jit(solution)/shard_map/all_to_all | solution.py:52
  243.1 0.6 fusion.3
  243.7 1.4 convolution_bitcast_fusion.3
  245.2 43.0 %all-reduce.21.cloned.1.call-done = f32[128,1024]{1,0:T(8,128)} async-done(((f32[128,1024]{1,0:T(8,128)}), f32[128,1024]{1,0:T(8,128)}) %all-reduce.21.cloned.1.call-update) | async-done | bytes 524304 | tf_op jit(solution)/shard_map/psum | solution.py:60
  288.2 1.5 fusion.43
  289.7 1.6 multiply_reduce_fusion.5
  291.2 9.6 %all-reduce.7 = (f32[]{:T(128)}, f32[]{:T(128)}, f32[]{:T(128)}) all-reduce(f32[]{:T(128)} %get-tuple-element.13, f32[]{:T(128)} %get-tuple-element.12, f32[]{:T(128)} %get-tuple-element.18), channel_id=1, replica_groups=mesh['cols'=4,'rows'=8] {'cols'}, use_global_device_ids=true, to_apply=%region_22.23 | all-reduce | flops 3 | bytes 24 | tf_op jit(solution)/shard_map/psum | solution.py:71
  300.9 14.4 %all-reduce.2 = (f32[]{:T(128)}, f32[]{:T(128)}, f32[]{:T(128)}) all-reduce(f32[]{:T(128)} %get-tuple-element.45, f32[]{:T(128)} %get-tuple-element.46, f32[]{:T(128)} %get-tuple-element.47), channel_id=1, replica_groups=mesh['cols'=4,'rows'=8] {'rows'}, use_global_device_ids=true, to_apply=%region_23.24 | all-reduce | flops 3 | bytes 24 | tf_op jit(solution)/shard_map/psum | solution.py:70
  317.3 0.6 gather_fusion.6
  317.8 8.3 %all_to_all.44 = bf16[32,8,128]{2,0,1:T(8,128)(2,1)S(1)} all-to-all(bf16[32,8,128]{2,0,1:T(8,128)(2,1)S(1)} %bitcast.345), channel_id=1, replica_groups=mesh['cols'=4,'rows'=8] {'rows'}, dimensions={1} | all-to-all | bytes 131072 | tf_op jit(solution)/shard_map/all_to_all | solution.py:52
  327.1 0.6 fusion.2
  327.7 1.4 convolution_bitcast_fusion.2
  329.2 43.0 %all-reduce.23.cloned.1.call-done = f32[128,1024]{1,0:T(8,128)} async-done(((f32[128,1024]{1,0:T(8,128)}), f32[128,1024]{1,0:T(8,128)}) %all-reduce.23.cloned.1.call-update) | async-done | bytes 524304 | tf_op jit(solution)/shard_map/psum | solution.py:60
  372.1 1.5 fusion.40
  373.6 1.6 fusion.13
  375.3 9.6 %all-reduce.6 = (f32[]{:T(128)}, f32[]{:T(128)}, f32[]{:T(128)}) all-reduce(f32[]{:T(128)} %get-tuple-element.17, f32[]{:T(128)} %get-tuple-element.16, f32[]{:T(128)} %get-tuple-element.15), channel_id=1, replica_groups=mesh['cols'=4,'rows'=8] {'cols'}, use_global_device_ids=true, to_apply=%region_32.33 | all-reduce | flops 3 | bytes 24 | tf_op jit(solution)/shard_map/psum | solution.py:71
  384.8 14.5 %all-reduce.1 = (f32[]{:T(128)}, f32[]{:T(128)}, f32[]{:T(128)}) all-reduce(f32[]{:T(128)} %get-tuple-element.42, f32[]{:T(128)} %get-tuple-element.43, f32[]{:T(128)} %get-tuple-element.44), channel_id=1, replica_groups=mesh['cols'=4,'rows'=8] {'rows'}, use_global_device_ids=true, to_apply=%region_33.34 | all-reduce | flops 3 | bytes 24 | tf_op jit(solution)/shard_map/psum | solution.py:70
  401.4 0.6 gather_fusion.8
  402.0 8.3 %all_to_all.45 = bf16[32,8,128]{2,0,1:T(8,128)(2,1)S(1)} all-to-all(bf16[32,8,128]{2,0,1:T(8,128)(2,1)S(1)} %bitcast.346), channel_id=1, replica_groups=mesh['cols'=4,'rows'=8] {'rows'}, dimensions={1} | all-to-all | bytes 131072 | tf_op jit(solution)/shard_map/all_to_all | solution.py:52
  411.2 0.6 fusion.1
  411.8 1.4 convolution_bitcast_fusion.1
  413.3 43.0 %all-reduce.25.cloned.1.call-done = f32[128,1024]{1,0:T(8,128)} async-done(((f32[128,1024]{1,0:T(8,128)}), f32[128,1024]{1,0:T(8,128)}) %all-reduce.25.cloned.1.call-update) | async-done | bytes 524304 | tf_op jit(solution)/shard_map/psum | solution.py:60
  456.3 1.5 fusion.37
  457.7 1.6 multiply_reduce_fusion.1
  459.3 9.6 %all-reduce.5 = (f32[]{:T(128)}, f32[]{:T(128)}, f32[]{:T(128)}) all-reduce(f32[]{:T(128)} %get-tuple-element.11, f32[]{:T(128)} %get-tuple-element.10, f32[]{:T(128)} %get-tuple-element.14), channel_id=1, replica_groups=mesh['cols'=4,'rows'=8] {'cols'}, use_global_device_ids=true, to_apply=%region_42.43 | all-reduce | flops 3 | bytes 24 | tf_op jit(solution)/shard_map/psum | solution.py:71
  468.9 14.5 %all-reduce = (f32[]{:T(128)}, f32[]{:T(128)}, f32[]{:T(128)}) all-reduce(f32[]{:T(128)} %get-tuple-element.39, f32[]{:T(128)} %get-tuple-element.40, f32[]{:T(128)} %get-tuple-element.41), channel_id=1, replica_groups=mesh['cols'=4,'rows'=8] {'rows'}, use_global_device_ids=true, to_apply=%region_43.44 | all-reduce | flops 3 | bytes 24 | tf_op jit(solution)/shard_map/psum | solution.py:70
  485.4 0.6 gather_fusion.10
  486.0 8.3 %all_to_all.46 = bf16[32,8,128]{2,0,1:T(8,128)(2,1)S(1)} all-to-all(bf16[32,8,128]{2,0,1:T(8,128)(2,1)S(1)} %bitcast.342), channel_id=1, replica_groups=mesh['cols'=4,'rows'=8] {'rows'}, dimensions={1} | all-to-all | bytes 131072 | tf_op jit(solution)/shard_map/all_to_all | solution.py:52
  495.2 0.6 fusion
  495.8 1.4 convolution_bitcast_fusion
  497.2 43.0 %all-reduce.27.cloned.1.call-done = f32[128,1024]{1,0:T(8,128)} async-done(((f32[128,1024]{1,0:T(8,128)}), f32[128,1024]{1,0:T(8,128)}) %all-reduce.27.cloned.1.call-update) | async-done | bytes 524304 | tf_op jit(solution)/shard_map/psum | solution.py:60
  540.3 1.5 multiply_reduce_fusion
  541.8 9.5 %psum.300 = f32[]{:T(128)} all-reduce(f32[]{:T(128)} %multiply_reduce_fusion), channel_id=1, replica_groups=mesh['cols'=4,'rows'=8] {'cols'}, use_global_device_ids=true, to_apply=%region_52.53 | all-reduce | flops 1 | bytes 8 | tf_op jit(solution)/shard_map/psum | solution.py:71
  551.4 14.4 %psum.301 = f32[]{:T(128)} all-reduce(f32[]{:T(128)} %psum.300), channel_id=1, replica_groups=mesh['cols'=4,'rows'=8] {'rows'}, use_global_device_ids=true, to_apply=%region_53.54 | all-reduce | flops 1 | bytes 8 | tf_op jit(solution)/shard_map/psum | solution.py:70
  566.5 0.7 fusion.35
  567.2 1.9 multiply_subtract_fusion
  (56 shorter events, 5.9 us)
Async XLA Ops:
  7.2 8.5 %copy-start = (f32[8,128,128]{2,1,0:T(8,128)S(1)}, f32[8,128,128]{2,1,0:T(8,128)}, u32[]{:S(2)}) copy-start(f32[8,128,128]{2,1,0:T(8,128)} %param.11) | copy-start | bytes 1572868
  7.9 0.7 copy-start.6
  9.3 11.9 %all-to-all-start = ((s32[8,1,1]{2,1,0:T(1,128)}), s32[8,1,1]{2,1,0:T(1,128)S(1)}, u32[]{:S(2)}, u32[]{:S(2)}) async-start(s32[8,1,1]{2,1,0:T(1,128)} %copy.175), calls=%async_computation | async-start | bytes 8192 | tf_op jit(solution)/shard_map/all_to_all | solution.py:35
  15.7 10.4 %copy-start.7 = (s32[4]{0:T(128)S(1)}, s32[4]{0:T(128)}, u32[]{:S(2)}) copy-start(s32[4]{0:T(128)} %param.13) | copy-start | bytes 52
  15.7 16.7 %copy-start.2 = (bf16[4,128,128]{2,1,0:T(8,128)(2,1)S(1)}, bf16[4,128,128]{2,1,0:T(8,128)(2,1)}, u32[]{:S(2)}) copy-start(bf16[4,128,128]{2,1,0:T(8,128)(2,1)} %param.12) | copy-start | bytes 393220
  17.2 15.6 %copy-start.1 = (f32[8,128,128]{2,1,0:T(8,128)S(1)}, f32[8,128,128]{2,1,0:T(8,128)}, u32[]{:S(2)}) copy-start(f32[8,128,128]{2,1,0:T(8,128)} %param.10) | copy-start | bytes 1572868
  22.6 9.2 %all-to-all-start.1 = ((bf16[32,8,128]{2,0,1:T(8,128)(2,1)}), bf16[32,8,128]{2,0,1:T(8,128)(2,1)S(1)}, u32[]{:S(2)}, u32[]{:S(2)}) async-start(bf16[32,8,128]{2,0,1:T(8,128)(2,1)} %bitcast.5), calls=%async_computation.1 | async-start | bytes 131072 | tf_op jit(solution)/shard_map/all_to_all | solution.py:52
  26.0 53.0 %all-reduce.17.cloned.1.call-start = ((), (), s32[]{:S(2)}) async-start(), calls=%async_computation.7 | async-start | bytes 1048576 | tf_op jit(solution)/shard_map/psum | solution.py:60
  32.8 0.7 copy-start.4
  35.0 170.0 %all-reduce.19.cloned.1.call-start = ((), (), s32[]{:S(2)}) async-start(), calls=%async_computation.8 | async-start | bytes 1048576 | tf_op jit(solution)/shard_map/psum | solution.py:60
  35.1 45.4 %copy-start.3 = (f32[32,1024]{1,0:T(8,128)S(1)}, f32[32,1024]{1,0:T(8,128)}, u32[]{:S(2)}) copy-start(f32[32,1024]{1,0:T(8,128)} %param.8) | copy-start | bytes 393220
  162.9 125.3 %all-reduce.21.cloned.1.call-start = ((), (), s32[]{:S(2)}) async-start(), calls=%async_computation.9 | async-start | bytes 1048576 | tf_op jit(solution)/shard_map/psum | solution.py:60
  205.0 1.5 copy-start.5
  245.2 127.0 %all-reduce.23.cloned.1.call-start = ((), (), s32[]{:S(2)}) async-start(), calls=%async_computation.10 | async-start | bytes 1048576 | tf_op jit(solution)/shard_map/psum | solution.py:60
  329.1 127.2 %all-reduce.25.cloned.1.call-start = ((), (), s32[]{:S(2)}) async-start(), calls=%async_computation.11 | async-start | bytes 1048576 | tf_op jit(solution)/shard_map/psum | solution.py:60
  413.2 127.0 %all-reduce.27.cloned.1.call-start = ((), (), s32[]{:S(2)}) async-start(), calls=%async_computation.12 | async-start | bytes 1048576 | tf_op jit(solution)/shard_map/psum | solution.py:60
Sparse Core Ops, SparseCore 0:
  35.1 43.8 all-reduce.16
  163.0 41.9 all-reduce.18
  245.3 42.8 all-reduce.20
  329.2 42.8 all-reduce.22
  413.4 42.8 all-reduce.24
  497.4 42.8 all-reduce.26
